TPU v7x, 128 devices: a whole 4x4x4 slice. The times are simulated.
128 devices in a mesh: song: 16 (over x_lo, z, core), tensor: 8 (over x_hi, y).
Axes of the slice: x: 4 (x_hi: 2, x_lo: 2; x = x_hi * 2 + x_lo), y: 4, z: 4, core: 2. Of those that a mesh axis runs over, the one named last changes fastest.
Arguments:
- upper_codes: int32 [4096], P('song'), may hold values from 0 to 2047
- middle_codes: int32 [16384], P('song'), may hold values from 0 to 2047
- upper_table: bfloat16 [2048, 1024], P(None, 'tensor'), may hold values from -6 to 6
- dilated_weight: bfloat16 [4, 3, 1024, 1024], P(None, None, 'tensor'), may hold values from -0.109375 to 0.109375
- mixing_weight: bfloat16 [4, 1024, 1024], P(None, None, 'tensor'), may hold values from -0.1875 to 0.1875
- upsample_weight: bfloat16 [1024, 7680], P('tensor'), may hold values from -0.1875 to 0.1875
- middle_table: bfloat16 [2048, 1920], P('tensor'), may hold values from -6 to 6
- norm_gain: float32 [1920], replicated, may hold values from 0.1 to 1.9
- qkv_weight: bfloat16 [1920, 16, 384], P(None, 'tensor'), may hold values from -4 to 4
Outputs:
- context: bfloat16 [16384, 2048], P('song', 'tensor')
All inputs are finite; a program needn't handle non-finite values.
Results may differ from a plain program's by a relative error of at most 0.0145.
Values may be sent and summed in bfloat16 or wider, within the bound.
No kernel may reach another device: no remote copies, remote signals or barrier semaphores. Data moves between devices by JAX's collectives and lax.ppermute only.
A program may use at most 128 MiB of HBM per device.

v0:
```python
import jax
import jax.numpy as jnp
from jax import lax
from jax.sharding import PartitionSpec as P

BLOCKS = 4


def extended(cells, sides, width):
    for axis, dim in sides:
        count = lax.axis_size(axis)
        ends = count - 1
        head = lax.slice_in_dim(cells, 0, width, axis=dim)
        tail = lax.slice_in_dim(cells, cells.shape[dim] - width, cells.shape[dim], axis=dim)
        cells = jnp.concatenate(
            [
                lax.ppermute(tail, axis, [(i, (i + 1) % count) for i in range(ends)]),
                cells,
                lax.ppermute(head, axis, [((i + 1) % count, i) for i in range(ends)]),
            ],
            axis=dim,
        )
    return cells


def from_behind(shard, axis, by):
    peers = lax.axis_size(axis)
    pairs = [(i, i + by) for i in range(peers) if 0 <= i + by < peers]
    return lax.ppermute(shard, axis, pairs)


def on_device(
    upper_codes,
    middle_codes,
    upper_table,
    dilated_weight,
    mixing_weight,
    upsample_weight,
    middle_table,
    norm_gain,
    qkv_weight,
):
    tensor_rank = lax.axis_index("tensor")
    song_rank = lax.axis_index("song")
    count = upper_codes.shape[0]
    rows = middle_codes.shape[0]
    width = norm_gain.shape[0]
    upper_vocab = upper_table.shape[0]
    upper_hot = (upper_codes[:, None] == jnp.arange(upper_vocab, dtype=jnp.int32)[None, :]).astype(
        jnp.bfloat16
    )
    state = jnp.dot(upper_hot, upper_table, preferred_element_type=jnp.float32)
    for level in range(BLOCKS):
        step = 3**level
        state_bf = jnp.maximum(state, 0.0).astype(jnp.bfloat16)
        padded = extended(state_bf, (("song", 0),), step)
        partial_value = jnp.dot(
            padded[0:count], dilated_weight[level, 0], preferred_element_type=jnp.float32
        )
        partial_value = partial_value + jnp.dot(
            padded[step : step + count],
            dilated_weight[level, 1],
            preferred_element_type=jnp.float32,
        )
        partial_value = partial_value + jnp.dot(
            padded[2 * step : 2 * step + count],
            dilated_weight[level, 2],
            preferred_element_type=jnp.float32,
        )
        summed = lax.psum(partial_value, "tensor")
        rect = jnp.maximum(summed, 0.0).astype(jnp.bfloat16)
        state = state + jnp.dot(rect, mixing_weight[level], preferred_element_type=jnp.float32)
    final = state.astype(jnp.bfloat16)
    vocab_rows = middle_table.shape[0]
    upsampled = jnp.dot(final, upsample_weight, preferred_element_type=jnp.float32).reshape(
        rows, width
    )
    local_codes = middle_codes - tensor_rank * vocab_rows
    middle_hot = (local_codes[:, None] == jnp.arange(vocab_rows, dtype=jnp.int32)[None, :]).astype(
        jnp.bfloat16
    )
    terms = upsampled + jnp.dot(middle_hot, middle_table, preferred_element_type=jnp.float32)
    frames = lax.psum(terms, "tensor")
    mean = jnp.mean(frames, axis=1, keepdims=True)
    var = jnp.mean((frames - mean) ** 2, axis=1, keepdims=True)
    normed = ((frames - mean) * lax.rsqrt(var + 1e-05) * norm_gain[None, :]).astype(jnp.bfloat16)
    heads_here = qkv_weight.shape[1]
    head_size = qkv_weight.shape[2] // 3
    projected = jnp.dot(
        normed,
        qkv_weight.reshape(width, heads_here * 3 * head_size),
        preferred_element_type=jnp.float32,
    )
    projected = projected.astype(jnp.bfloat16).reshape(rows, heads_here, 3 * head_size)
    queries = projected[:, :, 0:head_size]
    keys_own = projected[:, :, head_size : 2 * head_size].reshape(rows, heads_here * head_size)
    vals_own = projected[:, :, 2 * head_size : 3 * head_size].reshape(rows, heads_here * head_size)
    stacked = jnp.stack([keys_own, vals_own])
    near = from_behind(stacked, "song", 1)
    far = from_behind(stacked, "song", 2)
    every = jnp.concatenate([far, near, stacked], axis=1).reshape(
        2, 3 * rows, heads_here, head_size
    )
    all_keys = every[0]
    all_vals = every[1]
    scale = 1.0 / head_size**0.5
    key_rel = jnp.arange(3 * rows, dtype=jnp.int32) - 2 * rows
    lowest = -song_rank * rows
    span = min(rows, 512)
    outputs = []
    for begin in range(0, rows, span):
        q_blk = queries[begin : begin + span]
        scores = (
            jnp.einsum("qhd,khd->hqk", q_blk, all_keys, preferred_element_type=jnp.float32) * scale
        )
        query_pos = begin + jnp.arange(span, dtype=jnp.int32)
        valid = (key_rel[None, :] <= query_pos[:, None]) & (key_rel[None, :] >= lowest)
        scores = jnp.where(valid[None], scores, -1e30)
        top = jnp.max(scores, axis=-1, keepdims=True)
        expo = jnp.exp(scores - top)
        weights = (expo / jnp.sum(expo, axis=-1, keepdims=True)).astype(jnp.bfloat16)
        out = jnp.einsum("hqk,khd->qhd", weights, all_vals, preferred_element_type=jnp.float32)
        outputs.append(out.astype(jnp.bfloat16).reshape(span, heads_here * head_size))
    return jnp.concatenate(outputs, axis=0)


def solution(mesh):
    placed = (
        P("song"),
        P("song"),
        P(None, "tensor"),
        P(None, None, "tensor", None),
        P(None, None, "tensor"),
        P("tensor", None),
        P("tensor", None),
        P(),
        P(None, "tensor", None),
    )
    return jax.shard_map(
        on_device, mesh=mesh, in_specs=placed, out_specs=P("song", "tensor"), check_vma=False
    )
```

profile of v0, /device:TPU:3, one launch (start us, length us, event | category | flops | bytes accessed | tf_op | source)
XLA Modules:
  0.0 675.8 jit_solution(9196973381590233010)
XLA Ops:
  8.2 2.6 collective-permute-start.1
  10.8 3.4 collective-permute-start
  17.5 2.2 fusion.22
  19.7 68.5 %all-reduce.7 = bf16[256,1024]{1,0:T(8,128)(2,1)S(1)} all-reduce(f32[256,1024]{1,0:T(8,128)} %fusion.22), channel_id=1, replica_groups=mesh['song'=16,'tensor'=8] {'tensor'}, use_global_device_ids=true, to_apply=%region_0.0 | all-reduce | flops 262144 | bytes 1572864 | tf_op jit(solution)/shard_map/psum | solution.py:70
  90.1 17.1 %collective-permute-start.3 = (bf16[3,128]{1,0:T(4,128)(2,1)S(1)}, bf16[3,128]{1,0:T(4,128)(2,1)S(1)}, u32[]{:S(2)}, u32[]{:S(2)}) collective-permute-start(bf16[3,128]{1,0:T(4,128)(2,1)S(1)} %get-tuple-element.14), channel_id=1, source_target_pairs={{8,0},{16,8},{24,16},{32,24},{40,32},{48,40},{56,48},{64,56},{72,6... | collective-permute-start | bytes 2312 | tf_op jit(solution)/shard_map/ppermute | solution.py:19
  108.4 1.9 collective-permute-start.2
  112.8 64.1 %all-reduce.8 = bf16[256,1024]{1,0:T(8,128)(2,1)S(1)} all-reduce(f32[256,1024]{1,0:T(8,128)S(1)} %fusion.21), channel_id=1, replica_groups=mesh['song'=16,'tensor'=8] {'tensor'}, use_global_device_ids=true, to_apply=%region_1.0 | all-reduce | flops 262144 | bytes 1572864 | tf_op jit(solution)/shard_map/psum | solution.py:70
  176.9 1.9 maximum_convert_fusion.10
  178.8 16.9 %collective-permute-start.5 = (bf16[9,128]{1,0:T(8,128)(2,1)S(1)}, bf16[9,128]{1,0:T(8,128)(2,1)S(1)}, u32[]{:S(2)}, u32[]{:S(2)}) collective-permute-start(bf16[9,128]{1,0:T(8,128)(2,1)S(1)} %get-tuple-element.12), channel_id=1, source_target_pairs={{8,0},{16,8},{24,16},{32,24},{40,32},{48,40},{56,48},{64,56},{72,6... | collective-permute-start | bytes 6920 | tf_op jit(solution)/shard_map/ppermute | solution.py:19
  197.0 1.9 collective-permute-start.4
  201.4 67.9 %all-reduce.9 = bf16[256,1024]{1,0:T(8,128)(2,1)S(1)} all-reduce(f32[256,1024]{1,0:T(8,128)S(1)} %fusion.20), channel_id=1, replica_groups=mesh['song'=16,'tensor'=8] {'tensor'}, use_global_device_ids=true, to_apply=%region_2.0 | all-reduce | flops 262144 | bytes 1572864 | tf_op jit(solution)/shard_map/psum | solution.py:70
  269.3 1.9 maximum_convert_fusion.9
  271.2 17.1 %collective-permute-start.7 = (bf16[27,128]{1,0:T(8,128)(2,1)S(1)}, bf16[27,128]{1,0:T(8,128)(2,1)S(1)}, u32[]{:S(2)}, u32[]{:S(2)}) collective-permute-start(bf16[27,128]{1,0:T(8,128)(2,1)S(1)} %get-tuple-element.10), channel_id=1, source_target_pairs={{8,0},{16,8},{24,16},{32,24},{40,32},{48,40},{56,48},{64,56},{72,6... | collective-permute-start | bytes 20744 | tf_op jit(solution)/shard_map/ppermute | solution.py:19
  289.6 1.9 collective-permute-start.6
  294.0 64.3 %all-reduce.10 = bf16[256,1024]{1,0:T(8,128)(2,1)S(1)} all-reduce(f32[256,1024]{1,0:T(8,128)S(1)} %fusion.19), channel_id=1, replica_groups=mesh['song'=16,'tensor'=8] {'tensor'}, use_global_device_ids=true, to_apply=%region_3.0 | all-reduce | flops 262144 | bytes 1572864 | tf_op jit(solution)/shard_map/psum | solution.py:70
  358.3 5.5 fusion.30
  363.7 9.2 %reshape.128 = f32[1024,1920]{1,0:T(8,128)} reshape(f32[256,7680]{1,0:T(8,128)} %fusion.30) | data formatting | bytes 15728640 | tf_op jit(solution)/shard_map/reshape | solution.py:75
  373.0 7.7 %convolution_add_fusion = f32[1024,1920]{1,0:T(8,128)} fusion(f32[1024,1920]{1,0:T(8,128)} %reshape.128, bf16[256,1920]{1,0:T(8,128)(2,1)S(1)} %copy-done.6, s32[1024]{0:T(1024)S(1)} %broadcast_subtract_fusion), kind=kOutput, calls=%fused_computation.23 | convolution fusion | flops 1008861184 | bytes 16715776 | tf_op jit(solution)/shard_map/dot_general | solution.py:82
  380.7 4.0 copy.24
  384.7 184.2 %all-reduce.6.cloned.1.call-done = f32[1024,1920]{1,0:T(8,128)} async-done(((f32[1024,1920]{1,0:T(8,128)}), f32[1024,1920]{1,0:T(8,128)}) %all-reduce.6.cloned.1.call-update) | async-done | bytes 7864336 | tf_op jit(solution)/shard_map/psum | solution.py:83
  568.9 3.7 reduce_sum.36
  572.6 4.3 multiply_reduce_fusion
  578.0 5.8 fusion.18
  586.2 3.7 collective-permute-start.9
  589.9 3.2 collective-permute-start.8
  593.1 3.3 fusion.8
  596.4 14.2 %collective-permute-done.9 = bf16[2,1024,256]{1,2,0:T(8,128)(2,1)} collective-permute-done((bf16[2,1024,256]{1,2,0:T(8,128)(2,1)}, bf16[2,1024,256]{1,2,0:T(8,128)(2,1)}, u32[]{:S(2)}, u32[]{:S(2)}) %collective-permute-start.9) | collective-permute-done | bytes 1048608 | tf_op jit(solution)/shard_map/ppermute | solution.py:29
  610.6 16.5 %collective-permute-done.8 = bf16[2,1024,256]{1,2,0:T(8,128)(2,1)} collective-permute-done((bf16[2,1024,256]{1,2,0:T(8,128)(2,1)}, bf16[2,1024,256]{1,2,0:T(8,128)(2,1)}, u32[]{:S(2)}, u32[]{:S(2)}) %collective-permute-start.8) | collective-permute-done | bytes 1048608 | tf_op jit(solution)/shard_map/ppermute | solution.py:29
  631.1 10.8 %fusion.125 = (f32[2,512]{1,0:T(2,128)S(1)}, f32[2,512,3072]{2,1,0:T(8,128)}) fusion(pred[512,3072]{1,0:T(8,128)(4,1)S(1)} %copy-done.3, bf16[3072,2,128]{0,2,1:T(8,128)(2,1)} %bitcast.90, bf16[1024,2,384]{0,2,1:T(8,128)(2,1)} %bitcast.93), kind=kOutput, calls=%fused_computation.157 | convolution fusion | flops 817892352 | bytes 15994880 | tf_op jit(solution)/shard_map/sub | solution.py:120
  641.9 7.5 %fusion.27 = bf16[2,128,512]{2,1,0:T(8,128)(2,1)S(1)} fusion(bf16[3072,2,128]{0,2,1:T(8,128)(2,1)} %bitcast.88, f32[2,512,3072]{2,1,0:T(8,128)} %get-tuple-element.28, f32[2,512]{1,0:T(2,128)S(1)} %get-tuple-element.27), kind=kOutput, calls=%fused_computation.42 | convolution fusion | flops 811728896 | bytes 14422016 | tf_op jit(solution)/shard_map/hqk,khd->qhd/dot_general | solution.py:122
  650.2 10.3 %fusion.130 = (f32[2,512]{1,0:T(2,128)S(1)}, f32[2,512,3072]{2,1,0:T(8,128)}) fusion(pred[512,3072]{1,0:T(8,128)(4,1)S(1)} %get-tuple-element.17, bf16[3072,2,128]{0,2,1:T(8,128)(2,1)S(1)} %bitcast.91, bf16[1024,2,384]{0,2,1:T(8,128)(2,1)} %bitcast.94), kind=kOutput, calls=%fused_computation.158 | convolution fusion | flops 817892352 | bytes 15994880 | tf_op jit(solution)/shard_map/sub | solution.py:120
  660.5 7.5 %fusion.28 = bf16[2,128,512]{2,1,0:T(8,128)(2,1)S(1)} fusion(bf16[3072,2,128]{0,2,1:T(8,128)(2,1)} %bitcast.89, f32[2,512,3072]{2,1,0:T(8,128)} %get-tuple-element.30, f32[2,512]{1,0:T(2,128)S(1)} %get-tuple-element.29), kind=kOutput, calls=%fused_computation.43 | convolution fusion | flops 811728896 | bytes 14422016 | tf_op jit(solution)/shard_map/hqk,khd->qhd/dot_general | solution.py:122
  (58 shorter events, 27.2 us)
Async XLA Ops:
  6.5 351.7 %copy-start = (bf16[128,7680]{1,0:T(8,128)(2,1)S(1)}, bf16[128,7680]{1,0:T(8,128)(2,1)}, u32[]{:S(2)}) copy-start(bf16[128,7680]{1,0:T(8,128)(2,1)} %param.14) | copy-start | bytes 5898244
  6.5 562.4 %all-reduce.6.cloned.1.call-start = ((), (), s32[]{:S(2)}) async-start(), calls=%async_computation | async-start | bytes 15728640 | tf_op jit(solution)/shard_map/psum | solution.py:83
  8.2 8.0 %collective-permute-start.1 = (bf16[1,128]{1,0:T(2,128)(2,1)S(1)}, bf16[1,128]{1,0:T(2,128)(2,1)S(1)}, u32[]{:S(2)}, u32[]{:S(2)}) collective-permute-start(bf16[1,128]{1,0:T(2,128)(2,1)S(1)} %get-tuple-element.16), channel_id=1, source_target_pairs={{8,0},{16,8},{24,16},{32,24},{40,32},{48,40},{56,48},{64,56},{72,6... | collective-permute-start | bytes 776 | tf_op jit(solution)/shard_map/ppermute | solution.py:19
  10.8 6.6 collective-permute-start
  90.1 20.2 %collective-permute-start.3 = (bf16[3,128]{1,0:T(4,128)(2,1)S(1)}, bf16[3,128]{1,0:T(4,128)(2,1)S(1)}, u32[]{:S(2)}, u32[]{:S(2)}) collective-permute-start(bf16[3,128]{1,0:T(4,128)(2,1)S(1)} %get-tuple-element.14), channel_id=1, source_target_pairs={{8,0},{16,8},{24,16},{32,24},{40,32},{48,40},{56,48},{64,56},{72,6... | collective-permute-start | bytes 2312 | tf_op jit(solution)/shard_map/ppermute | solution.py:19
  108.4 3.2 collective-permute-start.2
  178.8 20.1 %collective-permute-start.5 = (bf16[9,128]{1,0:T(8,128)(2,1)S(1)}, bf16[9,128]{1,0:T(8,128)(2,1)S(1)}, u32[]{:S(2)}, u32[]{:S(2)}) collective-permute-start(bf16[9,128]{1,0:T(8,128)(2,1)S(1)} %get-tuple-element.12), channel_id=1, source_target_pairs={{8,0},{16,8},{24,16},{32,24},{40,32},{48,40},{56,48},{64,56},{72,6... | collective-permute-start | bytes 6920 | tf_op jit(solution)/shard_map/ppermute | solution.py:19
  197.0 3.2 collective-permute-start.4
  271.2 20.3 %collective-permute-start.7 = (bf16[27,128]{1,0:T(8,128)(2,1)S(1)}, bf16[27,128]{1,0:T(8,128)(2,1)S(1)}, u32[]{:S(2)}, u32[]{:S(2)}) collective-permute-start(bf16[27,128]{1,0:T(8,128)(2,1)S(1)} %get-tuple-element.10), channel_id=1, source_target_pairs={{8,0},{16,8},{24,16},{32,24},{40,32},{48,40},{56,48},{64,56},{72,6... | collective-permute-start | bytes 20744 | tf_op jit(solution)/shard_map/ppermute | solution.py:19
  289.6 3.2 collective-permute-start.6
  363.7 9.3 %copy-start.6 = (bf16[256,1920]{1,0:T(8,128)(2,1)S(1)}, bf16[256,1920]{1,0:T(8,128)(2,1)}, u32[]{:S(2)}) copy-start(bf16[256,1920]{1,0:T(8,128)(2,1)} %param.15) | copy-start | bytes 2949124
  572.6 5.5 copy-start.2
  572.6 5.5 copy-start.8
  583.8 1.2 copy-start.7
  586.2 24.5 %collective-permute-start.9 = (bf16[2,1024,256]{1,2,0:T(8,128)(2,1)}, bf16[2,1024,256]{1,2,0:T(8,128)(2,1)}, u32[]{:S(2)}, u32[]{:S(2)}) collective-permute-start(bf16[2,1024,256]{1,2,0:T(8,128)(2,1)} %pad_maximum_fusion), channel_id=1, source_target_pairs={{0,8},{8,16},{16,24},{24,32},{32,40},{40,48},{48,56},{56,64},{64,7... | collective-permute-start | bytes 3145736 | tf_op jit(solution)/shard_map/ppermute | solution.py:29
  589.9 37.2 %collective-permute-start.8 = (bf16[2,1024,256]{1,2,0:T(8,128)(2,1)}, bf16[2,1024,256]{1,2,0:T(8,128)(2,1)}, u32[]{:S(2)}, u32[]{:S(2)}) collective-permute-start(bf16[2,1024,256]{1,2,0:T(8,128)(2,1)} %pad_maximum_fusion), channel_id=1, source_target_pairs={{0,16},{8,24},{16,32},{24,40},{32,48},{40,56},{48,64},{56,72},{64,... | collective-permute-start | bytes 3145736 | tf_op jit(solution)/shard_map/ppermute | solution.py:29
  629.1 2.0 copy-start.3
  641.9 8.3 %copy-start.4 = (bf16[1,3072,256]{1,2,0:T(8,128)(2,1)S(1)}, bf16[1,3072,256]{1,2,0:T(8,128)(2,1)}, u32[]{:S(2)}) copy-start(bf16[1,3072,256]{1,2,0:T(8,128)(2,1)} %get-tuple-element.5) | copy-start | bytes 4718596
  660.5 7.6 %copy-start.5 = (bf16[512,256]{1,0:T(8,128)(2,1)S(1)}, bf16[512,256]{1,0:T(8,128)(2,1)}, u32[]{:S(2)}) copy-start(bf16[512,256]{1,0:T(8,128)(2,1)} %copy.19) | copy-start | bytes 786436
  660.5 8.5 %copy-start.1 = (bf16[128,7680]{1,0:T(8,128)(2,1)S(1)}, bf16[128,7680]{1,0:T(8,128)(2,1)}, u32[]{:S(2)}) copy-start(bf16[128,7680]{1,0:T(8,128)(2,1)} %param.14) | copy-start | bytes 5898244
Sparse Core Ops, SparseCore 0:
  380.8 188.0 all-reduce.5
where the time goes:
time: 677 us; the launch traced here: 676 us
  blocking collectives  265 us (39%)
  waiting for transfers between devices  215 us (32%)
  matrix products  78.2 us (12%)
  starting transfers between devices  69.8 us (10%)
  local copies, waits for them, and re-layouts  18.7 us (3%)
  other arithmetic  15.7 us (2%)
  between operations  13.8 us (2%)
    psum x4, blocking collectives, on_device(): summed = lax.psum(partial_value, 'tensor')  265 us
    psum x1, waiting for transfers between devices, on_device(): frames = lax.psum(terms, 'tensor')  184 us
    ppermute x4, starting transfers between devices, extended(): lax.ppermute(head, axis, [((i + 1) % count, i) for i in range(ends)])  53.6 us
    ppermute x2, waiting for transfers between devices, from_behind(): return lax.ppermute(shard, axis, pairs)  30.8 us
    sub x2, matrix products, on_device(): expo = jnp.exp(scores - top)  21.1 us
    dot_general x2, matrix products, on_device(): jnp.einsum('hqk,khd->qhd', weights, all_vals, preferred_element_type=jnp....  15 us
  transfers between devices with their start and end apart: 11, of which 3 were waited for; matrix products, arithmetic and copies ran while one was open for 3% of the time, Pallas kernels for 0%

commit v1 on v0

--- a/solution.py
+++ b/solution.py
@@ -67,7 +67,7 @@
             dilated_weight[level, 2],
             preferred_element_type=jnp.float32,
         )
-        summed = lax.psum(partial_value, "tensor")
+        summed = jnp.sum(lax.all_gather(partial_value, "tensor"), axis=0)
         rect = jnp.maximum(summed, 0.0).astype(jnp.bfloat16)
         state = state + jnp.dot(rect, mixing_weight[level], preferred_element_type=jnp.float32)
     final = state.astype(jnp.bfloat16)

time: 677 us -> 808 us (1.19)
  waiting for transfers between devices: 215 us -> 629 us
  blocking collectives: 265 us -> 0 us
  starting transfers between devices: 69.8 us -> 31.5 us
  other arithmetic: 15.7 us -> 32.7 us
    all_gather x0 -> x4, waiting for transfers between devices: none -> 425 us  [on_device(): summed = jnp.sum(lax.all_gather(partial_value, 'tensor'), axis=0)]
    psum x4 -> x0, blocking collectives: 265 us -> none  [on_device(): summed = lax.psum(partial_value, 'tensor')]
    ppermute x4, starting transfers between devices: 53.6 us -> 11.5 us  [extended(): lax.ppermute(head, axis, [((i + 1) % count, i) for i in range(ends)])]
    reduce_sum x0 -> x4, other arithmetic: none -> 17.6 us  [on_device(): summed = jnp.sum(lax.all_gather(partial_value, 'tensor'), axis=0)]
    psum x1, waiting for transfers between devices: 184 us -> 170 us  [on_device(): frames = lax.psum(terms, 'tensor')]
  transfers between devices with their start and end apart: 11 -> 15, of which waited for: 3 -> 10; matrix products, arithmetic and copies ran while one was open for 3% -> 2% of each run, Pallas kernels for 0% -> 0%
where the time goes in v1:
time: 808 us; the launch traced here: 807 us
  waiting for transfers between devices  629 us (78%)
  matrix products  81.2 us (10%)
  other arithmetic  32.7 us (4%)
  starting transfers between devices  31.5 us (4%)
  local copies, waits for them, and re-layouts  18.7 us (2%)
  between operations  13.5 us (2%)
    all_gather x4, waiting for transfers between devices, on_device(): summed = jnp.sum(lax.all_gather(partial_value, 'tensor'), axis=0)  425 us
    psum x1, waiting for transfers between devices, on_device(): frames = lax.psum(terms, 'tensor')  170 us
    ppermute x2, waiting for transfers between devices, from_behind(): return lax.ppermute(shard, axis, pairs)  30.7 us
    sub x2, matrix products, on_device(): expo = jnp.exp(scores - top)  21 us
    reduce_sum x4, other arithmetic, on_device(): summed = jnp.sum(lax.all_gather(partial_value, 'tensor'), axis=0)  17.6 us
  transfers between devices with their start and end apart: 15, of which 10 were waited for; matrix products, arithmetic and copies ran while one was open for 2% of the time, Pallas kernels for 0%

profile of v1, /device:TPU:3, one launch (start us, length us, event | category | flops | bytes accessed | tf_op | source)
XLA Modules:
  0.0 806.7 jit_solution(6649281607524657382)
XLA Ops:
  11.5 3.4 collective-permute-start
  19.8 109.2 %all-gather.9.cloned.1.call-done = f32[2048,1024]{1,0:T(8,128)} async-done(((f32[256,1024]{1,0:T(8,128)}), f32[2048,1024]{1,0:T(8,128)}) %all-gather.9.cloned.1.call-update) | async-done | bytes 8388624 | tf_op jit(solution)/shard_map/all_gather | solution.py:70
  129.0 4.5 reduce_sum.72
  135.4 3.0 collective-permute-start.3
  139.6 3.1 collective-permute-start.2
  147.4 105.2 %all-gather.11.cloned.1.call-done = f32[2048,1024]{1,0:T(8,128)} async-done(((f32[256,1024]{1,0:T(8,128)}), f32[2048,1024]{1,0:T(8,128)}) %all-gather.11.cloned.1.call-update) | async-done | bytes 8388624 | tf_op jit(solution)/shard_map/all_gather | solution.py:70
  252.6 4.4 reduce_sum.73
  258.8 3.0 collective-permute-start.5
  263.0 3.1 collective-permute-start.4
  270.8 105.2 %all-gather.13.cloned.1.call-done = f32[2048,1024]{1,0:T(8,128)} async-done(((f32[256,1024]{1,0:T(8,128)}), f32[2048,1024]{1,0:T(8,128)}) %all-gather.13.cloned.1.call-update) | async-done | bytes 8388624 | tf_op jit(solution)/shard_map/all_gather | solution.py:70
  376.0 4.4 reduce_sum.74
  381.7 3.0 collective-permute-start.7
  385.9 3.1 collective-permute-start.6
  393.9 105.0 %all-gather.15.cloned.1.call-done = f32[2048,1024]{1,0:T(8,128)} async-done(((f32[256,1024]{1,0:T(8,128)}), f32[2048,1024]{1,0:T(8,128)}) %all-gather.15.cloned.1.call-update) | async-done | bytes 8388624 | tf_op jit(solution)/shard_map/all_gather | solution.py:70
  499.0 4.4 reduce_sum.75
  503.4 5.4 fusion.30
  508.8 9.2 %reshape.128 = f32[1024,1920]{1,0:T(8,128)} reshape(f32[256,7680]{1,0:T(8,128)} %fusion.30) | data formatting | bytes 15728640 | tf_op jit(solution)/shard_map/reshape | solution.py:75
  518.0 7.7 convolution_add_fusion
  525.7 4.0 copy.24
  529.8 170.4 %all-reduce.2.cloned.1.call-done = f32[1024,1920]{1,0:T(8,128)} async-done(((f32[1024,1920]{1,0:T(8,128)}), f32[1024,1920]{1,0:T(8,128)}) %all-reduce.2.cloned.1.call-update) | async-done | bytes 7864336 | tf_op jit(solution)/shard_map/psum | solution.py:83
  700.2 3.7 reduce_sum.76
  703.8 4.3 multiply_reduce_fusion
  709.3 5.8 fusion.18
  717.4 3.7 collective-permute-start.9
  721.2 3.2 collective-permute-start.8
  724.4 3.3 fusion.8
  727.7 14.2 %collective-permute-done.9 = bf16[2,1024,256]{1,2,0:T(8,128)(2,1)} collective-permute-done((bf16[2,1024,256]{1,2,0:T(8,128)(2,1)}, bf16[2,1024,256]{1,2,0:T(8,128)(2,1)}, u32[]{:S(2)}, u32[]{:S(2)}) %collective-permute-start.9) | collective-permute-done | bytes 1048608 | tf_op jit(solution)/shard_map/ppermute | solution.py:29
  741.9 16.5 %collective-permute-done.8 = bf16[2,1024,256]{1,2,0:T(8,128)(2,1)} collective-permute-done((bf16[2,1024,256]{1,2,0:T(8,128)(2,1)}, bf16[2,1024,256]{1,2,0:T(8,128)(2,1)}, u32[]{:S(2)}, u32[]{:S(2)}) %collective-permute-start.8) | collective-permute-done | bytes 1048608 | tf_op jit(solution)/shard_map/ppermute | solution.py:29
  762.4 10.8 %fusion.125 = (f32[2,512]{1,0:T(2,128)S(1)}, f32[2,512,3072]{2,1,0:T(8,128)}) fusion(pred[512,3072]{1,0:T(8,128)(4,1)S(1)} %copy-done.3, bf16[3072,2,128]{0,2,1:T(8,128)(2,1)} %bitcast.98, bf16[1024,2,384]{0,2,1:T(8,128)(2,1)} %bitcast.101), kind=kOutput, calls=%fused_computation.157 | convolution fusion | flops 817892352 | bytes 15994880 | tf_op jit(solution)/shard_map/sub | solution.py:120
  773.1 7.5 fusion.27
  781.5 10.2 %fusion.130 = (f32[2,512]{1,0:T(2,128)S(1)}, f32[2,512,3072]{2,1,0:T(8,128)}) fusion(pred[512,3072]{1,0:T(8,128)(4,1)S(1)} %get-tuple-element.17, bf16[3072,2,128]{0,2,1:T(8,128)(2,1)S(1)} %bitcast.99, bf16[1024,2,384]{0,2,1:T(8,128)(2,1)} %bitcast.102), kind=kOutput, calls=%fused_computation.158 | convolution fusion | flops 817892352 | bytes 15994880 | tf_op jit(solution)/shard_map/sub | solution.py:120
  791.7 7.5 fusion.28
  (76 shorter events, 41.9 us)
Async XLA Ops:
  6.5 496.8 %copy-start = (bf16[128,7680]{1,0:T(8,128)(2,1)S(1)}, bf16[128,7680]{1,0:T(8,128)(2,1)}, u32[]{:S(2)}) copy-start(bf16[128,7680]{1,0:T(8,128)(2,1)} %param.14) | copy-start | bytes 5898244
  6.5 122.5 %all-gather.9.cloned.1.call-start = ((), (), s32[]{:S(2)}) async-start(), calls=%async_computation.1 | async-start | bytes 9437184 | tf_op jit(solution)/shard_map/all_gather | solution.py:70
  8.9 7.3 collective-permute-start.1
  11.5 6.0 collective-permute-start
  19.7 232.8 %all-gather.11.cloned.1.call-start = ((), (), s32[]{:S(2)}) async-start(), calls=%async_computation.2 | async-start | bytes 9437184 | tf_op jit(solution)/shard_map/all_gather | solution.py:70
  129.0 4.5 copy-start.8
  135.4 7.3 collective-permute-start.3
  139.6 5.4 collective-permute-start.2
  147.3 228.7 %all-gather.13.cloned.1.call-start = ((), (), s32[]{:S(2)}) async-start(), calls=%async_computation.3 | async-start | bytes 9437184 | tf_op jit(solution)/shard_map/all_gather | solution.py:70
  258.8 7.3 collective-permute-start.5
  263.0 5.4 collective-permute-start.4
  270.8 228.2 %all-gather.15.cloned.1.call-start = ((), (), s32[]{:S(2)}) async-start(), calls=%async_computation.4 | async-start | bytes 9437184 | tf_op jit(solution)/shard_map/all_gather | solution.py:70
  376.0 4.4 copy-start.11
  381.7 7.3 collective-permute-start.7
  385.9 8.0 copy-start.9
  385.9 5.4 collective-permute-start.6
  393.7 306.5 %all-reduce.2.cloned.1.call-start = ((), (), s32[]{:S(2)}) async-start(), calls=%async_computation | async-start | bytes 15728640 | tf_op jit(solution)/shard_map/psum | solution.py:83
  508.8 9.3 %copy-start.6 = (bf16[256,1920]{1,0:T(8,128)(2,1)S(1)}, bf16[256,1920]{1,0:T(8,128)(2,1)}, u32[]{:S(2)}) copy-start(bf16[256,1920]{1,0:T(8,128)(2,1)} %param.15) | copy-start | bytes 2949124
  703.8 5.5 copy-start.2
  703.8 5.5 copy-start.10
  715.1 1.2 copy-start.7
  717.4 24.5 %collective-permute-start.9 = (bf16[2,1024,256]{1,2,0:T(8,128)(2,1)}, bf16[2,1024,256]{1,2,0:T(8,128)(2,1)}, u32[]{:S(2)}, u32[]{:S(2)}) collective-permute-start(bf16[2,1024,256]{1,2,0:T(8,128)(2,1)} %pad_maximum_fusion), channel_id=1, source_target_pairs={{0,8},{8,16},{16,24},{24,32},{32,40},{40,48},{48,56},{56,64},{64,7... | collective-permute-start | bytes 3145736 | tf_op jit(solution)/shard_map/ppermute | solution.py:29
  721.2 37.2 %collective-permute-start.8 = (bf16[2,1024,256]{1,2,0:T(8,128)(2,1)}, bf16[2,1024,256]{1,2,0:T(8,128)(2,1)}, u32[]{:S(2)}, u32[]{:S(2)}) collective-permute-start(bf16[2,1024,256]{1,2,0:T(8,128)(2,1)} %pad_maximum_fusion), channel_id=1, source_target_pairs={{0,16},{8,24},{16,32},{24,40},{32,48},{40,56},{48,64},{56,72},{64,... | collective-permute-start | bytes 3145736 | tf_op jit(solution)/shard_map/ppermute | solution.py:29
  760.3 2.0 copy-start.3
  773.1 8.3 %copy-start.4 = (bf16[1,3072,256]{1,2,0:T(8,128)(2,1)S(1)}, bf16[1,3072,256]{1,2,0:T(8,128)(2,1)}, u32[]{:S(2)}) copy-start(bf16[1,3072,256]{1,2,0:T(8,128)(2,1)} %get-tuple-element.5) | copy-start | bytes 4718596
  791.7 7.6 copy-start.5
  791.7 8.5 %copy-start.1 = (bf16[128,7680]{1,0:T(8,128)(2,1)S(1)}, bf16[128,7680]{1,0:T(8,128)(2,1)}, u32[]{:S(2)}) copy-start(bf16[128,7680]{1,0:T(8,128)(2,1)} %param.14) | copy-start | bytes 5898244
Sparse Core Ops, SparseCore 0:
  19.9 109.1 all-gather.8
  147.4 105.0 all-gather.10
  270.9 105.0 all-gather.12
  393.8 105.1 all-gather.14
  525.8 174.2 all-reduce.1
